TPU v7x, 32 devices: a whole 2x2x4 slice. The times are simulated.
32 devices in a mesh: layer: 8 (over z, x), tile: 4 (over y, core).
Axes of the slice: x: 2, y: 2, z: 4, core: 2. Of those that a mesh axis runs over, the one named last changes fastest.
Arguments:
- source_modes: bfloat16 [8, 8, 2, 32, 512], P('layer', None, None, 'tile'), may hold values from -6 to 6
- port_cells: int32 [8], replicated, may hold values from 0 to 511
- frequencies: float32 [2], replicated, may hold values from 0.3 to 1.5, as said below
- layer_inverse: bfloat16 [8, 2, 32, 512, 512], P('layer', None, 'tile'), may hold values from -0.092807765 to 1.6928078
- coupling_self: float32 [8, 2, 32, 512], P('layer', None, 'tile'), may hold values from 0.4 to 1
- coupling_curl: float32 [8, 2, 32, 512], P('layer', None, 'tile'), may hold values from -4 to 4
Outputs:
- snapshot_basis: float32 [8, 32, 2, 32, 512], P('layer', None, None, 'tile')
- triangle: float32 [32, 32], replicated
Inputs may be any that keep to these rules, and one draw needn't show every extreme that they name: `port_cells`: each port's profile is centred on this plane column. `frequencies`: the second frequency is 1.5 to 2.5 times the first.
All inputs are finite; a program needn't handle non-finite values.
Results may differ from a plain program's by a relative error of at most 0.04.
Values may be sent and summed in bfloat16 or wider, within the bound.
A program may use at most 64 MiB of HBM per device.

v0:
```python
import jax
import jax.numpy as jnp
from jax import lax
from jax.sharding import PartitionSpec as P


def with_halo(cells, sides, width):
    for axis, dim in sides:
        count = lax.axis_size(axis)
        ends = count - 1
        head = lax.slice_in_dim(cells, 0, width, axis=dim)
        tail = lax.slice_in_dim(cells, cells.shape[dim] - width, cells.shape[dim], axis=dim)
        cells = jnp.concatenate(
            [
                lax.ppermute(tail, axis, [(i, (i + 1) % count) for i in range(ends)]),
                cells,
                lax.ppermute(head, axis, [((i + 1) % count, i) for i in range(ends)]),
            ],
            axis=dim,
        )
    return cells


def shifted(array, axis, by):
    size = lax.axis_size(axis)
    pairs = [(i, i + by) for i in range(size) if 0 <= i + by < size]
    return lax.ppermute(array, axis, pairs)


def lower_factor(gram):
    order = gram.shape[0]
    index_row = jnp.arange(order)

    def column_step(col_no, lower):
        unit = (index_row == col_no).astype(gram.dtype)
        column = jnp.dot(gram, unit, precision=lax.Precision.HIGHEST)
        lower_row = jnp.dot(unit, lower, precision=lax.Precision.HIGHEST)
        column = column - jnp.dot(lower, lower_row, precision=lax.Precision.HIGHEST)
        pivot = jnp.sqrt(jnp.sum(column * unit))
        scaled = jnp.where(index_row >= col_no, column / pivot, 0.0)
        return lower + scaled[:, None] * unit[None, :]

    return lax.fori_loop(0, order, column_step, jnp.zeros_like(gram))


def lower_inverse(lower):
    order = lower.shape[0]
    index_row = jnp.arange(order)

    def row_step(row_no, inverse):
        unit = (index_row == row_no).astype(lower.dtype)
        lower_row = jnp.dot(unit, lower, precision=lax.Precision.HIGHEST)
        pivot = jnp.sum(lower_row * unit)
        new_row = (unit - jnp.dot(lower_row, inverse, precision=lax.Precision.HIGHEST)) / pivot
        return inverse + unit[:, None] * new_row[None, :]

    return lax.fori_loop(0, order, row_step, jnp.zeros_like(lower))


def per_device(source_modes, port_cells, frequencies, layer_inverse, coupling_self, coupling_curl):
    layers_total = lax.axis_size("layer")
    tile_count = lax.axis_size("tile")
    layer_pos = lax.axis_index("layer")
    inverse_block = layer_inverse[0]
    self_w = coupling_self[0]
    curl_w = coupling_curl[0]
    rows_dev = source_modes.shape[3]
    plane_width = source_modes.shape[4]
    columns = jnp.arange(plane_width, dtype=jnp.float32)
    offsets = (columns[None, :] - port_cells.astype(jnp.float32)[:, None]) / (plane_width // 8)
    port_taper = 1.0 / (1.0 + offsets * offsets)
    phase_angle = frequencies * (layer_pos + 1).astype(jnp.float32)
    phase_pair = jnp.stack([jnp.cos(phase_angle), jnp.sin(phase_angle)], axis=1)
    source_layer = source_modes[0].astype(jnp.float32)
    forcing = (
        source_layer[:, None, None]
        * port_taper[:, None, None, None, None, :]
        * phase_pair[None, :, :, None, None, None]
    )
    forcing = forcing.reshape((-1, 2, rows_dev, plane_width))
    column_total = forcing.shape[0]
    group_count = 4
    group_width = column_total // group_count
    forcing_groups = forcing.reshape(group_count, group_width, 2, rows_dev, plane_width)
    step_count = layers_total + group_count - 1

    def couple(field):
        x_part = field[:, 0].astype(jnp.float32)
        y_part = field[:, 1].astype(jnp.float32)
        rim_rows = with_halo(y_part, (("tile", 1),), 1)
        row_diff = rim_rows[:, 2:] - rim_rows[:, :-2]
        cols_pad = jnp.pad(x_part, ((0, 0), (0, 0), (1, 1)))
        col_diff = cols_pad[:, :, 2:] - cols_pad[:, :, :-2]
        part_one = self_w[0] * x_part + curl_w[0] * row_diff
        part_two = self_w[1] * y_part + curl_w[1] * col_diff
        return jnp.stack([part_one, part_two], axis=1)

    def apply_inverse(vectors):
        return jnp.einsum(
            "crik,jcrk->jcri", inverse_block, vectors, preferred_element_type=jnp.float32
        )

    store_shape = (group_count, group_width, 2, rows_dev, plane_width)
    group_shape = (group_width, 2, rows_dev, plane_width)

    def down_step(step_no, state_pair):
        stored, incoming = state_pair
        group_no = jnp.clip(step_no - layer_pos, 0, group_count - 1)
        forcing_now = lax.dynamic_index_in_dim(forcing_groups, group_no, 0, keepdims=False)
        residue = (forcing_now - couple(incoming)).astype(jnp.bfloat16)
        current = apply_inverse(residue).astype(jnp.bfloat16)
        stored = lax.dynamic_update_index_in_dim(stored, current, group_no, 0)
        incoming = shifted(current, "layer", 1)
        return (stored, incoming)

    down_store, _ = lax.fori_loop(
        0,
        step_count,
        down_step,
        (jnp.zeros(store_shape, jnp.bfloat16), jnp.zeros(group_shape, jnp.bfloat16)),
    )
    reverse_pos = layers_total - 1 - layer_pos

    def up_step(step_no, state_pair):
        stored, incoming = state_pair
        group_no = jnp.clip(step_no - reverse_pos, 0, group_count - 1)
        earlier = lax.dynamic_index_in_dim(down_store, group_no, 0, keepdims=False)
        up_image = couple(incoming).astype(jnp.bfloat16)
        current = earlier.astype(jnp.float32) - apply_inverse(up_image)
        stored = lax.dynamic_update_index_in_dim(stored, current, group_no, 0)
        incoming = shifted(current, "layer", -1)
        return (stored, incoming)

    up_store, _ = lax.fori_loop(
        0,
        step_count,
        up_step,
        (jnp.zeros(store_shape, jnp.float32), jnp.zeros(group_shape, jnp.float32)),
    )
    columns_mat = up_store.reshape(column_total, -1)
    gram_local = jnp.dot(columns_mat, columns_mat.T, precision=lax.Precision.HIGHEST)
    total_rows = layers_total * tile_count * columns_mat.shape[1]
    gram_whole = lax.psum(gram_local, ("layer", "tile"))
    triangle = lower_factor(gram_whole / total_rows).T
    solved = jnp.dot(lower_inverse(triangle.T), columns_mat, precision=lax.Precision.HIGHEST)
    basis_out = solved.reshape(1, column_total, 2, rows_dev, plane_width)
    return (basis_out, triangle)


def solution(mesh):
    in_specs = (
        P("layer", None, None, "tile", None),
        P(),
        P(),
        P("layer", None, "tile", None, None),
        P("layer", None, "tile", None),
        P("layer", None, "tile", None),
    )
    out_specs = (P("layer", None, None, "tile", None), P())
    return jax.shard_map(
        per_device, mesh=mesh, in_specs=in_specs, out_specs=out_specs, check_vma=False
    )
```

profile of v0, /device:TPU:0, one launch (start us, length us, event | category | flops | bytes accessed | tf_op | source)
XLA Modules:
  0.0 634.1 jit_solution(17380595981949021285)
XLA Ops:
  3.6 223.6 %while.63 = (s32[]{:T(128)}, bf16[4,8,2,8,512]{4,1,3,2,0:T(8,128)(2,1)S(1)}, bf16[8,2,8,512]{3,0,2,1:T(8,128)(2,1)S(1)}, s32[]{:T(128)}, f32[4,8,2,8,512]{4,3,2,...) while((s32[]{:T(128)}, ...), condition=%wide.region_1.2_spmd, body=%wide.region_0.1_spmd.sunk | while | flops 67829760 | bytes 11698449 | solution.py:116
  11.4 5.7 bitcast_dynamic-update-slice_fusion.4
  30.1 5.7 bitcast_dynamic-update-slice_fusion.4
  35.8 4.4 collective-permute-start.2
  49.8 5.7 bitcast_dynamic-update-slice_fusion.4
  55.5 4.4 collective-permute-start.2
  69.5 5.7 bitcast_dynamic-update-slice_fusion.4
  75.2 5.3 collective-permute-start.2
  90.1 5.7 bitcast_dynamic-update-slice_fusion.4
  95.8 5.3 collective-permute-start.2
  110.7 5.7 bitcast_dynamic-update-slice_fusion.4
  116.4 5.3 collective-permute-start.2
  131.3 5.7 bitcast_dynamic-update-slice_fusion.4
  137.0 5.3 collective-permute-start.2
  151.9 5.7 bitcast_dynamic-update-slice_fusion.4
  157.6 5.3 collective-permute-start.2
  172.5 5.7 bitcast_dynamic-update-slice_fusion.4
  178.2 5.3 collective-permute-start.2
  193.1 5.7 bitcast_dynamic-update-slice_fusion.4
  198.8 5.3 collective-permute-start.2
  213.7 5.7 bitcast_dynamic-update-slice_fusion.4
  219.4 5.3 collective-permute-start.2
  227.3 250.6 %while.64 = (s32[]{:T(128)}, f32[4,8,2,8,512]{4,1,3,2,0:T(8,128)S(1)}, f32[8,2,8,512]{3,0,2,1:T(8,128)S(1)}, s32[]{:T(128)}, bf16[4,8,2,8,512]{4,1,3,2,0:T(8,128...) while((s32[]{:T(128)}, ...), condition=%wide.region_3.4_spmd, body=%wide.region_2.3_spmd.sunk | while | flops 67698688 | bytes 11829517 | solution.py:134
  234.5 5.7 bitcast_dynamic-update-slice_fusion.5
  241.4 9.3 %collective-permute-done.5 = f32[8,2,8,512]{3,0,2,1:T(8,128)S(1)} collective-permute-done((f32[8,2,8,512]{3,0,2,1:T(8,128)S(1)}, f32[8,2,8,512]{3,0,2,1:T(8,128)S(1)}, u32[]{:S(2)}, u32[]{:S(2)}) %collective-permute-start.5) | collective-permute-done | bytes 262176 | tf_op jit(solution)/shard_map/while/body/eval_jaxpr/ppermute | solution.py:27
  257.5 5.7 bitcast_dynamic-update-slice_fusion.5
  264.5 9.6 %collective-permute-done.5 = f32[8,2,8,512]{3,0,2,1:T(8,128)S(1)} collective-permute-done((f32[8,2,8,512]{3,0,2,1:T(8,128)S(1)}, f32[8,2,8,512]{3,0,2,1:T(8,128)S(1)}, u32[]{:S(2)}, u32[]{:S(2)}) %collective-permute-start.5) | collective-permute-done | bytes 262176 | tf_op jit(solution)/shard_map/while/body/eval_jaxpr/ppermute | solution.py:27
  280.6 5.7 bitcast_dynamic-update-slice_fusion.5
  287.6 9.4 %collective-permute-done.5 = f32[8,2,8,512]{3,0,2,1:T(8,128)S(1)} collective-permute-done((f32[8,2,8,512]{3,0,2,1:T(8,128)S(1)}, f32[8,2,8,512]{3,0,2,1:T(8,128)S(1)}, u32[]{:S(2)}, u32[]{:S(2)}) %collective-permute-start.5) | collective-permute-done | bytes 262176 | tf_op jit(solution)/shard_map/while/body/eval_jaxpr/ppermute | solution.py:27
  303.2 5.7 bitcast_dynamic-update-slice_fusion.5
  310.2 9.4 %collective-permute-done.5 = f32[8,2,8,512]{3,0,2,1:T(8,128)S(1)} collective-permute-done((f32[8,2,8,512]{3,0,2,1:T(8,128)S(1)}, f32[8,2,8,512]{3,0,2,1:T(8,128)S(1)}, u32[]{:S(2)}, u32[]{:S(2)}) %collective-permute-start.5) | collective-permute-done | bytes 262176 | tf_op jit(solution)/shard_map/while/body/eval_jaxpr/ppermute | solution.py:27
  325.9 5.7 bitcast_dynamic-update-slice_fusion.5
  332.8 9.4 %collective-permute-done.5 = f32[8,2,8,512]{3,0,2,1:T(8,128)S(1)} collective-permute-done((f32[8,2,8,512]{3,0,2,1:T(8,128)S(1)}, f32[8,2,8,512]{3,0,2,1:T(8,128)S(1)}, u32[]{:S(2)}, u32[]{:S(2)}) %collective-permute-start.5) | collective-permute-done | bytes 262176 | tf_op jit(solution)/shard_map/while/body/eval_jaxpr/ppermute | solution.py:27
  348.5 5.7 bitcast_dynamic-update-slice_fusion.5
  355.4 9.4 %collective-permute-done.5 = f32[8,2,8,512]{3,0,2,1:T(8,128)S(1)} collective-permute-done((f32[8,2,8,512]{3,0,2,1:T(8,128)S(1)}, f32[8,2,8,512]{3,0,2,1:T(8,128)S(1)}, u32[]{:S(2)}, u32[]{:S(2)}) %collective-permute-start.5) | collective-permute-done | bytes 262176 | tf_op jit(solution)/shard_map/while/body/eval_jaxpr/ppermute | solution.py:27
  371.1 5.7 bitcast_dynamic-update-slice_fusion.5
  378.1 9.4 %collective-permute-done.5 = f32[8,2,8,512]{3,0,2,1:T(8,128)S(1)} collective-permute-done((f32[8,2,8,512]{3,0,2,1:T(8,128)S(1)}, f32[8,2,8,512]{3,0,2,1:T(8,128)S(1)}, u32[]{:S(2)}, u32[]{:S(2)}) %collective-permute-start.5) | collective-permute-done | bytes 262176 | tf_op jit(solution)/shard_map/while/body/eval_jaxpr/ppermute | solution.py:27
  393.7 5.7 bitcast_dynamic-update-slice_fusion.5
  400.7 9.4 %collective-permute-done.5 = f32[8,2,8,512]{3,0,2,1:T(8,128)S(1)} collective-permute-done((f32[8,2,8,512]{3,0,2,1:T(8,128)S(1)}, f32[8,2,8,512]{3,0,2,1:T(8,128)S(1)}, u32[]{:S(2)}, u32[]{:S(2)}) %collective-permute-start.5) | collective-permute-done | bytes 262176 | tf_op jit(solution)/shard_map/while/body/eval_jaxpr/ppermute | solution.py:27
  416.4 5.7 bitcast_dynamic-update-slice_fusion.5
  423.3 9.4 %collective-permute-done.5 = f32[8,2,8,512]{3,0,2,1:T(8,128)S(1)} collective-permute-done((f32[8,2,8,512]{3,0,2,1:T(8,128)S(1)}, f32[8,2,8,512]{3,0,2,1:T(8,128)S(1)}, u32[]{:S(2)}, u32[]{:S(2)}) %collective-permute-start.5) | collective-permute-done | bytes 262176 | tf_op jit(solution)/shard_map/while/body/eval_jaxpr/ppermute | solution.py:27
  439.0 5.7 bitcast_dynamic-update-slice_fusion.5
  445.9 9.4 %collective-permute-done.5 = f32[8,2,8,512]{3,0,2,1:T(8,128)S(1)} collective-permute-done((f32[8,2,8,512]{3,0,2,1:T(8,128)S(1)}, f32[8,2,8,512]{3,0,2,1:T(8,128)S(1)}, u32[]{:S(2)}, u32[]{:S(2)}) %collective-permute-start.5) | collective-permute-done | bytes 262176 | tf_op jit(solution)/shard_map/while/body/eval_jaxpr/ppermute | solution.py:27
  461.6 5.7 bitcast_dynamic-update-slice_fusion.5
  468.6 9.4 %collective-permute-done.5 = f32[8,2,8,512]{3,0,2,1:T(8,128)S(1)} collective-permute-done((f32[8,2,8,512]{3,0,2,1:T(8,128)S(1)}, f32[8,2,8,512]{3,0,2,1:T(8,128)S(1)}, u32[]{:S(2)}, u32[]{:S(2)}) %collective-permute-start.5) | collective-permute-done | bytes 262176 | tf_op jit(solution)/shard_map/while/body/eval_jaxpr/ppermute | solution.py:27
  478.9 41.6 %psum.7 = f32[32,32]{1,0:T(8,128)S(1)} all-reduce(f32[32,32]{1,0:T(8,128)S(1)} %fusion.62), channel_id=1, replica_groups=mesh['layer'=8,'tile'=4] {'layer','tile'}, use_global_device_ids=true, to_apply=%region_4.5 | all-reduce | flops 1024 | bytes 8192 | tf_op jit(solution)/shard_map/psum | solution.py:143
  520.5 58.2 %while.66 = (s32[]{:T(128)}, f32[32,32]{1,0:T(8,128)S(1)}, f32[32,32]{1,0:T(8,128)S(1)}, s32[]{:T(128)}, s32[]{:T(128)}) while((s32[]{:T(128)}, f32[32,32]{1,0:T(8,128)S(1)}, f32[32,32]{1,0:T(8,128)S(1)}, s32[]{:T(128)}, s32[]{:T(128)}) %tuple.180), condition=%wide.region_7.8_spmd.clone.clone, body=%wide.region_5.7_spmd.clone.clone.sunk | while | flops 42338 | bytes 21869 | solution.py:43
  578.7 50.9 %while.65 = (s32[]{:T(128)}, f32[32,32]{1,0:T(8,128)S(1)}, f32[32,32]{1,0:T(8,128)S(1)}, s32[]{:T(128)}, s32[]{:T(128)}) while((s32[]{:T(128)}, f32[32,32]{1,0:T(8,128)S(1)}, f32[32,32]{1,0:T(8,128)S(1)}, s32[]{:T(128)}, s32[]{:T(128)}) %tuple.183), condition=%wide.region_10.11_spmd.clone, body=%wide.region_8.10_spmd.clone.sunk | while | flops 28994 | bytes 17244 | solution.py:57
  (552 shorter events, 289.4 us)
Async XLA Ops:
  3.6 4.5 collective-permute-start
  6.0 5.2 collective-permute-start.1
  17.0 5.9 collective-permute-start.2
  23.0 5.6 collective-permute-start
  26.5 3.5 collective-permute-start.1
  35.8 6.9 %collective-permute-start.2 = (bf16[8,2,8,512]{3,0,2,1:T(8,128)(2,1)S(1)}, bf16[8,2,8,512]{3,0,2,1:T(8,128)(2,1)S(1)}, u32[]{:S(2)}, u32[]{:S(2)}) collective-permute-start(bf16[8,2,8,512]{3,0,2,1:T(8,128)(2,1)S(1)} %bitcast.184), channel_id=1, source_target_pairs={{0,4},{4,8},{8,12},{12,16},{16,20},{20,24},{24,28},{1,5},{5,9},{9,... | collective-permute-start | bytes 393224 | tf_op jit(solution)/shard_map/while/body/eval_jaxpr/ppermute | solution.py:27
  42.7 5.6 collective-permute-start
  55.5 6.9 %collective-permute-start.2 = (bf16[8,2,8,512]{3,0,2,1:T(8,128)(2,1)S(1)}, bf16[8,2,8,512]{3,0,2,1:T(8,128)(2,1)S(1)}, u32[]{:S(2)}, u32[]{:S(2)}) collective-permute-start(bf16[8,2,8,512]{3,0,2,1:T(8,128)(2,1)S(1)} %bitcast.184), channel_id=1, source_target_pairs={{0,4},{4,8},{8,12},{12,16},{16,20},{20,24},{24,28},{1,5},{5,9},{9,... | collective-permute-start | bytes 393224 | tf_op jit(solution)/shard_map/while/body/eval_jaxpr/ppermute | solution.py:27
  62.4 5.6 collective-permute-start
  65.9 3.5 collective-permute-start.1
  75.2 7.8 %collective-permute-start.2 = (bf16[8,2,8,512]{3,0,2,1:T(8,128)(2,1)S(1)}, bf16[8,2,8,512]{3,0,2,1:T(8,128)(2,1)S(1)}, u32[]{:S(2)}, u32[]{:S(2)}) collective-permute-start(bf16[8,2,8,512]{3,0,2,1:T(8,128)(2,1)S(1)} %bitcast.184), channel_id=1, source_target_pairs={{0,4},{4,8},{8,12},{12,16},{16,20},{20,24},{24,28},{1,5},{5,9},{9,... | collective-permute-start | bytes 393224 | tf_op jit(solution)/shard_map/while/body/eval_jaxpr/ppermute | solution.py:27
  83.0 5.6 collective-permute-start
  95.8 7.8 %collective-permute-start.2 = (bf16[8,2,8,512]{3,0,2,1:T(8,128)(2,1)S(1)}, bf16[8,2,8,512]{3,0,2,1:T(8,128)(2,1)S(1)}, u32[]{:S(2)}, u32[]{:S(2)}) collective-permute-start(bf16[8,2,8,512]{3,0,2,1:T(8,128)(2,1)S(1)} %bitcast.184), channel_id=1, source_target_pairs={{0,4},{4,8},{8,12},{12,16},{16,20},{20,24},{24,28},{1,5},{5,9},{9,... | collective-permute-start | bytes 393224 | tf_op jit(solution)/shard_map/while/body/eval_jaxpr/ppermute | solution.py:27
  103.6 5.6 collective-permute-start
  116.4 7.8 %collective-permute-start.2 = (bf16[8,2,8,512]{3,0,2,1:T(8,128)(2,1)S(1)}, bf16[8,2,8,512]{3,0,2,1:T(8,128)(2,1)S(1)}, u32[]{:S(2)}, u32[]{:S(2)}) collective-permute-start(bf16[8,2,8,512]{3,0,2,1:T(8,128)(2,1)S(1)} %bitcast.184), channel_id=1, source_target_pairs={{0,4},{4,8},{8,12},{12,16},{16,20},{20,24},{24,28},{1,5},{5,9},{9,... | collective-permute-start | bytes 393224 | tf_op jit(solution)/shard_map/while/body/eval_jaxpr/ppermute | solution.py:27
  124.2 5.6 collective-permute-start
  127.7 3.5 collective-permute-start.1
  137.0 7.8 %collective-permute-start.2 = (bf16[8,2,8,512]{3,0,2,1:T(8,128)(2,1)S(1)}, bf16[8,2,8,512]{3,0,2,1:T(8,128)(2,1)S(1)}, u32[]{:S(2)}, u32[]{:S(2)}) collective-permute-start(bf16[8,2,8,512]{3,0,2,1:T(8,128)(2,1)S(1)} %bitcast.184), channel_id=1, source_target_pairs={{0,4},{4,8},{8,12},{12,16},{16,20},{20,24},{24,28},{1,5},{5,9},{9,... | collective-permute-start | bytes 393224 | tf_op jit(solution)/shard_map/while/body/eval_jaxpr/ppermute | solution.py:27
  144.8 5.6 collective-permute-start
  157.6 7.8 %collective-permute-start.2 = (bf16[8,2,8,512]{3,0,2,1:T(8,128)(2,1)S(1)}, bf16[8,2,8,512]{3,0,2,1:T(8,128)(2,1)S(1)}, u32[]{:S(2)}, u32[]{:S(2)}) collective-permute-start(bf16[8,2,8,512]{3,0,2,1:T(8,128)(2,1)S(1)} %bitcast.184), channel_id=1, source_target_pairs={{0,4},{4,8},{8,12},{12,16},{16,20},{20,24},{24,28},{1,5},{5,9},{9,... | collective-permute-start | bytes 393224 | tf_op jit(solution)/shard_map/while/body/eval_jaxpr/ppermute | solution.py:27
  165.4 5.6 collective-permute-start
  178.2 7.8 %collective-permute-start.2 = (bf16[8,2,8,512]{3,0,2,1:T(8,128)(2,1)S(1)}, bf16[8,2,8,512]{3,0,2,1:T(8,128)(2,1)S(1)}, u32[]{:S(2)}, u32[]{:S(2)}) collective-permute-start(bf16[8,2,8,512]{3,0,2,1:T(8,128)(2,1)S(1)} %bitcast.184), channel_id=1, source_target_pairs={{0,4},{4,8},{8,12},{12,16},{16,20},{20,24},{24,28},{1,5},{5,9},{9,... | collective-permute-start | bytes 393224 | tf_op jit(solution)/shard_map/while/body/eval_jaxpr/ppermute | solution.py:27
  186.0 5.6 collective-permute-start
  198.8 7.8 %collective-permute-start.2 = (bf16[8,2,8,512]{3,0,2,1:T(8,128)(2,1)S(1)}, bf16[8,2,8,512]{3,0,2,1:T(8,128)(2,1)S(1)}, u32[]{:S(2)}, u32[]{:S(2)}) collective-permute-start(bf16[8,2,8,512]{3,0,2,1:T(8,128)(2,1)S(1)} %bitcast.184), channel_id=1, source_target_pairs={{0,4},{4,8},{8,12},{12,16},{16,20},{20,24},{24,28},{1,5},{5,9},{9,... | collective-permute-start | bytes 393224 | tf_op jit(solution)/shard_map/while/body/eval_jaxpr/ppermute | solution.py:27
  206.6 5.6 collective-permute-start
  219.4 7.8 %collective-permute-start.2 = (bf16[8,2,8,512]{3,0,2,1:T(8,128)(2,1)S(1)}, bf16[8,2,8,512]{3,0,2,1:T(8,128)(2,1)S(1)}, u32[]{:S(2)}, u32[]{:S(2)}) collective-permute-start(bf16[8,2,8,512]{3,0,2,1:T(8,128)(2,1)S(1)} %bitcast.184), channel_id=1, source_target_pairs={{0,4},{4,8},{8,12},{12,16},{16,20},{20,24},{24,28},{1,5},{5,9},{9,... | collective-permute-start | bytes 393224 | tf_op jit(solution)/shard_map/while/body/eval_jaxpr/ppermute | solution.py:27
  227.3 5.6 collective-permute-start.3
  240.1 10.6 %collective-permute-start.5 = (f32[8,2,8,512]{3,0,2,1:T(8,128)S(1)}, f32[8,2,8,512]{3,0,2,1:T(8,128)S(1)}, u32[]{:S(2)}, u32[]{:S(2)}) collective-permute-start(f32[8,2,8,512]{3,0,2,1:T(8,128)S(1)} %get-tuple-element.874), channel_id=1, source_target_pairs={{4,0},{8,4},{12,8},{16,12},{20,16},{24,20},{28,24},{5,1},{9,5},{13... | collective-permute-start | bytes 786440 | tf_op jit(solution)/shard_map/while/body/eval_jaxpr/ppermute | solution.py:27
  250.8 5.6 collective-permute-start.3
  263.2 11.0 %collective-permute-start.5 = (f32[8,2,8,512]{3,0,2,1:T(8,128)S(1)}, f32[8,2,8,512]{3,0,2,1:T(8,128)S(1)}, u32[]{:S(2)}, u32[]{:S(2)}) collective-permute-start(f32[8,2,8,512]{3,0,2,1:T(8,128)S(1)} %get-tuple-element.874), channel_id=1, source_target_pairs={{4,0},{8,4},{12,8},{16,12},{20,16},{24,20},{28,24},{5,1},{9,5},{13... | collective-permute-start | bytes 786440 | tf_op jit(solution)/shard_map/while/body/eval_jaxpr/ppermute | solution.py:27
  274.2 5.3 collective-permute-start.3
  286.3 10.7 %collective-permute-start.5 = (f32[8,2,8,512]{3,0,2,1:T(8,128)S(1)}, f32[8,2,8,512]{3,0,2,1:T(8,128)S(1)}, u32[]{:S(2)}, u32[]{:S(2)}) collective-permute-start(f32[8,2,8,512]{3,0,2,1:T(8,128)S(1)} %get-tuple-element.874), channel_id=1, source_target_pairs={{4,0},{8,4},{12,8},{16,12},{20,16},{24,20},{28,24},{5,1},{9,5},{13... | collective-permute-start | bytes 786440 | tf_op jit(solution)/shard_map/while/body/eval_jaxpr/ppermute | solution.py:27
  297.0 5.1 collective-permute-start.3
  308.9 10.7 %collective-permute-start.5 = (f32[8,2,8,512]{3,0,2,1:T(8,128)S(1)}, f32[8,2,8,512]{3,0,2,1:T(8,128)S(1)}, u32[]{:S(2)}, u32[]{:S(2)}) collective-permute-start(f32[8,2,8,512]{3,0,2,1:T(8,128)S(1)} %get-tuple-element.874), channel_id=1, source_target_pairs={{4,0},{8,4},{12,8},{16,12},{20,16},{24,20},{28,24},{5,1},{9,5},{13... | collective-permute-start | bytes 786440 | tf_op jit(solution)/shard_map/while/body/eval_jaxpr/ppermute | solution.py:27
  319.6 5.1 collective-permute-start.3
  331.5 10.7 %collective-permute-start.5 = (f32[8,2,8,512]{3,0,2,1:T(8,128)S(1)}, f32[8,2,8,512]{3,0,2,1:T(8,128)S(1)}, u32[]{:S(2)}, u32[]{:S(2)}) collective-permute-start(f32[8,2,8,512]{3,0,2,1:T(8,128)S(1)} %get-tuple-element.874), channel_id=1, source_target_pairs={{4,0},{8,4},{12,8},{16,12},{20,16},{24,20},{28,24},{5,1},{9,5},{13... | collective-permute-start | bytes 786440 | tf_op jit(solution)/shard_map/while/body/eval_jaxpr/ppermute | solution.py:27
  342.2 5.1 collective-permute-start.3
  354.1 10.7 %collective-permute-start.5 = (f32[8,2,8,512]{3,0,2,1:T(8,128)S(1)}, f32[8,2,8,512]{3,0,2,1:T(8,128)S(1)}, u32[]{:S(2)}, u32[]{:S(2)}) collective-permute-start(f32[8,2,8,512]{3,0,2,1:T(8,128)S(1)} %get-tuple-element.874), channel_id=1, source_target_pairs={{4,0},{8,4},{12,8},{16,12},{20,16},{24,20},{28,24},{5,1},{9,5},{13... | collective-permute-start | bytes 786440 | tf_op jit(solution)/shard_map/while/body/eval_jaxpr/ppermute | solution.py:27
  364.8 5.1 collective-permute-start.3
  376.8 10.7 %collective-permute-start.5 = (f32[8,2,8,512]{3,0,2,1:T(8,128)S(1)}, f32[8,2,8,512]{3,0,2,1:T(8,128)S(1)}, u32[]{:S(2)}, u32[]{:S(2)}) collective-permute-start(f32[8,2,8,512]{3,0,2,1:T(8,128)S(1)} %get-tuple-element.874), channel_id=1, source_target_pairs={{4,0},{8,4},{12,8},{16,12},{20,16},{24,20},{28,24},{5,1},{9,5},{13... | collective-permute-start | bytes 786440 | tf_op jit(solution)/shard_map/while/body/eval_jaxpr/ppermute | solution.py:27
  387.5 5.1 collective-permute-start.3
  399.4 10.7 %collective-permute-start.5 = (f32[8,2,8,512]{3,0,2,1:T(8,128)S(1)}, f32[8,2,8,512]{3,0,2,1:T(8,128)S(1)}, u32[]{:S(2)}, u32[]{:S(2)}) collective-permute-start(f32[8,2,8,512]{3,0,2,1:T(8,128)S(1)} %get-tuple-element.874), channel_id=1, source_target_pairs={{4,0},{8,4},{12,8},{16,12},{20,16},{24,20},{28,24},{5,1},{9,5},{13... | collective-permute-start | bytes 786440 | tf_op jit(solution)/shard_map/while/body/eval_jaxpr/ppermute | solution.py:27
  410.1 5.1 collective-permute-start.3
  422.0 10.7 %collective-permute-start.5 = (f32[8,2,8,512]{3,0,2,1:T(8,128)S(1)}, f32[8,2,8,512]{3,0,2,1:T(8,128)S(1)}, u32[]{:S(2)}, u32[]{:S(2)}) collective-permute-start(f32[8,2,8,512]{3,0,2,1:T(8,128)S(1)} %get-tuple-element.874), channel_id=1, source_target_pairs={{4,0},{8,4},{12,8},{16,12},{20,16},{24,20},{28,24},{5,1},{9,5},{13... | collective-permute-start | bytes 786440 | tf_op jit(solution)/shard_map/while/body/eval_jaxpr/ppermute | solution.py:27
  432.7 5.1 collective-permute-start.3
  444.6 10.7 %collective-permute-start.5 = (f32[8,2,8,512]{3,0,2,1:T(8,128)S(1)}, f32[8,2,8,512]{3,0,2,1:T(8,128)S(1)}, u32[]{:S(2)}, u32[]{:S(2)}) collective-permute-start(f32[8,2,8,512]{3,0,2,1:T(8,128)S(1)} %get-tuple-element.874), channel_id=1, source_target_pairs={{4,0},{8,4},{12,8},{16,12},{20,16},{24,20},{28,24},{5,1},{9,5},{13... | collective-permute-start | bytes 786440 | tf_op jit(solution)/shard_map/while/body/eval_jaxpr/ppermute | solution.py:27
  455.3 5.1 collective-permute-start.3
  467.3 10.7 %collective-permute-start.5 = (f32[8,2,8,512]{3,0,2,1:T(8,128)S(1)}, f32[8,2,8,512]{3,0,2,1:T(8,128)S(1)}, u32[]{:S(2)}, u32[]{:S(2)}) collective-permute-start(f32[8,2,8,512]{3,0,2,1:T(8,128)S(1)} %get-tuple-element.874), channel_id=1, source_target_pairs={{4,0},{8,4},{12,8},{16,12},{20,16},{24,20},{28,24},{5,1},{9,5},{13... | collective-permute-start | bytes 786440 | tf_op jit(solution)/shard_map/while/body/eval_jaxpr/ppermute | solution.py:27
  (18 other events, 58.5 us)
where the time goes:
time: 640 us; the launch traced here: 634 us
  matrix products  208 us (32%)
  starting transfers between devices  169 us (26%)
  waiting for transfers between devices  159 us (25%)
  blocking collectives  41.6 us (6%)
  loops' own time  24 us (4%)
  local copies, waits for them, and re-layouts  21 us (3%)
  other arithmetic  11.1 us (2%)
    ppermute x22, waiting for transfers between devices, shifted(): return lax.ppermute(array, axis, pairs)  131 us
    dot_general x22, matrix products, apply_inverse(): jnp.einsum('crik,jcrk->jcri', inverse_block, vectors, preferred_element_t...  124 us
    ppermute x22, starting transfers between devices, with_halo(): lax.ppermute(tail, axis, [(i, (i + 1) % count) for i in range(ends)])  72.2 us
    ppermute x22, starting transfers between devices, shifted(): return lax.ppermute(array, axis, pairs)  68.5 us
    psum x1, blocking collectives, per_device(): gram_whole = lax.psum(gram_local, ('layer', 'tile'))  41.6 us
    ppermute x22, starting transfers between devices, with_halo(): lax.ppermute(head, axis, [((i + 1) % count, i) for i in range(ends)])  28.4 us
    ppermute x22, waiting for transfers between devices, with_halo(): lax.ppermute(head, axis, [((i + 1) % count, i) for i in range(ends)])  27.9 us
    dot_general x32, matrix products, column_step(): column = column - jnp.dot(lower, lower_row, precision=lax.Precision.HIGHEST)  24.9 us
  transfers between devices with their start and end apart: 66, of which 44 were waited for; matrix products, arithmetic and copies ran while one was open for 3% of the time, Pallas kernels for 0%

commit v1 on v0

--- a/solution.py
+++ b/solution.py
@@ -140,7 +140,7 @@
     columns_mat = up_store.reshape(column_total, -1)
     gram_local = jnp.dot(columns_mat, columns_mat.T, precision=lax.Precision.HIGHEST)
     total_rows = layers_total * tile_count * columns_mat.shape[1]
-    gram_whole = lax.psum(gram_local, ("layer", "tile"))
+    gram_whole = jax.lax.psum(jax.lax.psum(gram_local, axis_name="tile"), axis_name="layer")
     triangle = lower_factor(gram_whole / total_rows).T
     solved = jnp.dot(lower_inverse(triangle.T), columns_mat, precision=lax.Precision.HIGHEST)
     basis_out = solved.reshape(1, column_total, 2, rows_dev, plane_width)

time: 640 us -> 645 us (level)
    psum x1 -> x2, blocking collectives: 41.6 us -> 47.1 us  [the longest x1 36 us: per_device(): jax.lax.psum(jax.lax.psum(gram_local, axis_name='tile'), axis_name='layer')]
where the time goes in v1:
time: 645 us; the launch traced here: 640 us
  matrix products  208 us (32%)
  starting transfers between devices  169 us (26%)
  waiting for transfers between devices  159 us (25%)
  blocking collectives  47.1 us (7%)
  loops' own time  24 us (4%)
  local copies, waits for them, and re-layouts  21 us (3%)
  other arithmetic  11.2 us (2%)
    ppermute x22, waiting for transfers between devices, shifted(): return lax.ppermute(array, axis, pairs)  131 us
    dot_general x22, matrix products, apply_inverse(): jnp.einsum('crik,jcrk->jcri', inverse_block, vectors, preferred_element_t...  124 us
    ppermute x22, starting transfers between devices, with_halo(): lax.ppermute(tail, axis, [(i, (i + 1) % count) for i in range(ends)])  72.2 us
    ppermute x22, starting transfers between devices, shifted(): return lax.ppermute(array, axis, pairs)  68.5 us
    psum x1, blocking collectives, per_device(): jax.lax.psum(jax.lax.psum(gram_local, axis_name='tile'), axis_name='layer')  36 us
    ppermute x22, starting transfers between devices, with_halo(): lax.ppermute(head, axis, [((i + 1) % count, i) for i in range(ends)])  28.4 us
    ppermute x22, waiting for transfers between devices, with_halo(): lax.ppermute(head, axis, [((i + 1) % count, i) for i in range(ends)])  27.9 us
    dot_general x32, matrix products, column_step(): column = column - jnp.dot(lower, lower_row, precision=lax.Precision.HIGHEST)  24.9 us
  transfers between devices with their start and end apart: 66, of which 44 were waited for; matrix products, arithmetic and copies ran while one was open for 3% of the time, Pallas kernels for 0%

profile of v1, /device:TPU:0, one launch (start us, length us, event | category | flops | bytes accessed | tf_op | source)
XLA Modules:
  0.0 639.6 jit_solution(15160661912539070682)
XLA Ops:
  3.6 223.6 %while.63 = (s32[]{:T(128)}, bf16[4,8,2,8,512]{4,1,3,2,0:T(8,128)(2,1)S(1)}, bf16[8,2,8,512]{3,0,2,1:T(8,128)(2,1)S(1)}, s32[]{:T(128)}, f32[4,8,2,8,512]{4,3,2,...) while((s32[]{:T(128)}, ...), condition=%wide.region_1.2_spmd, body=%wide.region_0.1_spmd.sunk | while | flops 67829760 | bytes 11698449 | solution.py:116
  11.4 5.7 bitcast_dynamic-update-slice_fusion.4
  30.1 5.7 bitcast_dynamic-update-slice_fusion.4
  49.8 5.7 bitcast_dynamic-update-slice_fusion.4
  55.5 4.4 collective-permute-start.2
  69.5 5.7 bitcast_dynamic-update-slice_fusion.4
  75.2 5.3 collective-permute-start.2
  90.1 5.7 bitcast_dynamic-update-slice_fusion.4
  95.8 5.3 collective-permute-start.2
  110.7 5.7 bitcast_dynamic-update-slice_fusion.4
  116.4 5.3 collective-permute-start.2
  131.3 5.7 bitcast_dynamic-update-slice_fusion.4
  137.0 5.3 collective-permute-start.2
  151.9 5.7 bitcast_dynamic-update-slice_fusion.4
  157.6 5.3 collective-permute-start.2
  172.5 5.7 bitcast_dynamic-update-slice_fusion.4
  178.2 5.3 collective-permute-start.2
  193.1 5.7 bitcast_dynamic-update-slice_fusion.4
  198.8 5.3 collective-permute-start.2
  213.7 5.7 bitcast_dynamic-update-slice_fusion.4
  219.4 5.3 collective-permute-start.2
  227.3 250.6 %while.64 = (s32[]{:T(128)}, f32[4,8,2,8,512]{4,1,3,2,0:T(8,128)S(1)}, f32[8,2,8,512]{3,0,2,1:T(8,128)S(1)}, s32[]{:T(128)}, bf16[4,8,2,8,512]{4,1,3,2,0:T(8,128...) while((s32[]{:T(128)}, ...), condition=%wide.region_3.4_spmd, body=%wide.region_2.3_spmd.sunk | while | flops 67698688 | bytes 11829517 | solution.py:134
  234.5 5.7 bitcast_dynamic-update-slice_fusion.5
  241.4 9.3 %collective-permute-done.5 = f32[8,2,8,512]{3,0,2,1:T(8,128)S(1)} collective-permute-done((f32[8,2,8,512]{3,0,2,1:T(8,128)S(1)}, f32[8,2,8,512]{3,0,2,1:T(8,128)S(1)}, u32[]{:S(2)}, u32[]{:S(2)}) %collective-permute-start.5) | collective-permute-done | bytes 262176 | tf_op jit(solution)/shard_map/while/body/eval_jaxpr/ppermute | solution.py:27
  257.5 5.7 bitcast_dynamic-update-slice_fusion.5
  264.5 9.6 %collective-permute-done.5 = f32[8,2,8,512]{3,0,2,1:T(8,128)S(1)} collective-permute-done((f32[8,2,8,512]{3,0,2,1:T(8,128)S(1)}, f32[8,2,8,512]{3,0,2,1:T(8,128)S(1)}, u32[]{:S(2)}, u32[]{:S(2)}) %collective-permute-start.5) | collective-permute-done | bytes 262176 | tf_op jit(solution)/shard_map/while/body/eval_jaxpr/ppermute | solution.py:27
  280.6 5.7 bitcast_dynamic-update-slice_fusion.5
  287.6 9.4 %collective-permute-done.5 = f32[8,2,8,512]{3,0,2,1:T(8,128)S(1)} collective-permute-done((f32[8,2,8,512]{3,0,2,1:T(8,128)S(1)}, f32[8,2,8,512]{3,0,2,1:T(8,128)S(1)}, u32[]{:S(2)}, u32[]{:S(2)}) %collective-permute-start.5) | collective-permute-done | bytes 262176 | tf_op jit(solution)/shard_map/while/body/eval_jaxpr/ppermute | solution.py:27
  303.2 5.7 bitcast_dynamic-update-slice_fusion.5
  310.2 9.4 %collective-permute-done.5 = f32[8,2,8,512]{3,0,2,1:T(8,128)S(1)} collective-permute-done((f32[8,2,8,512]{3,0,2,1:T(8,128)S(1)}, f32[8,2,8,512]{3,0,2,1:T(8,128)S(1)}, u32[]{:S(2)}, u32[]{:S(2)}) %collective-permute-start.5) | collective-permute-done | bytes 262176 | tf_op jit(solution)/shard_map/while/body/eval_jaxpr/ppermute | solution.py:27
  325.9 5.7 bitcast_dynamic-update-slice_fusion.5
  332.8 9.4 %collective-permute-done.5 = f32[8,2,8,512]{3,0,2,1:T(8,128)S(1)} collective-permute-done((f32[8,2,8,512]{3,0,2,1:T(8,128)S(1)}, f32[8,2,8,512]{3,0,2,1:T(8,128)S(1)}, u32[]{:S(2)}, u32[]{:S(2)}) %collective-permute-start.5) | collective-permute-done | bytes 262176 | tf_op jit(solution)/shard_map/while/body/eval_jaxpr/ppermute | solution.py:27
  348.5 5.7 bitcast_dynamic-update-slice_fusion.5
  355.4 9.4 %collective-permute-done.5 = f32[8,2,8,512]{3,0,2,1:T(8,128)S(1)} collective-permute-done((f32[8,2,8,512]{3,0,2,1:T(8,128)S(1)}, f32[8,2,8,512]{3,0,2,1:T(8,128)S(1)}, u32[]{:S(2)}, u32[]{:S(2)}) %collective-permute-start.5) | collective-permute-done | bytes 262176 | tf_op jit(solution)/shard_map/while/body/eval_jaxpr/ppermute | solution.py:27
  371.1 5.7 bitcast_dynamic-update-slice_fusion.5
  378.1 9.4 %collective-permute-done.5 = f32[8,2,8,512]{3,0,2,1:T(8,128)S(1)} collective-permute-done((f32[8,2,8,512]{3,0,2,1:T(8,128)S(1)}, f32[8,2,8,512]{3,0,2,1:T(8,128)S(1)}, u32[]{:S(2)}, u32[]{:S(2)}) %collective-permute-start.5) | collective-permute-done | bytes 262176 | tf_op jit(solution)/shard_map/while/body/eval_jaxpr/ppermute | solution.py:27
  393.7 5.7 bitcast_dynamic-update-slice_fusion.5
  400.7 9.4 %collective-permute-done.5 = f32[8,2,8,512]{3,0,2,1:T(8,128)S(1)} collective-permute-done((f32[8,2,8,512]{3,0,2,1:T(8,128)S(1)}, f32[8,2,8,512]{3,0,2,1:T(8,128)S(1)}, u32[]{:S(2)}, u32[]{:S(2)}) %collective-permute-start.5) | collective-permute-done | bytes 262176 | tf_op jit(solution)/shard_map/while/body/eval_jaxpr/ppermute | solution.py:27
  416.4 5.7 bitcast_dynamic-update-slice_fusion.5
  423.3 9.4 %collective-permute-done.5 = f32[8,2,8,512]{3,0,2,1:T(8,128)S(1)} collective-permute-done((f32[8,2,8,512]{3,0,2,1:T(8,128)S(1)}, f32[8,2,8,512]{3,0,2,1:T(8,128)S(1)}, u32[]{:S(2)}, u32[]{:S(2)}) %collective-permute-start.5) | collective-permute-done | bytes 262176 | tf_op jit(solution)/shard_map/while/body/eval_jaxpr/ppermute | solution.py:27
  439.0 5.7 bitcast_dynamic-update-slice_fusion.5
  445.9 9.4 %collective-permute-done.5 = f32[8,2,8,512]{3,0,2,1:T(8,128)S(1)} collective-permute-done((f32[8,2,8,512]{3,0,2,1:T(8,128)S(1)}, f32[8,2,8,512]{3,0,2,1:T(8,128)S(1)}, u32[]{:S(2)}, u32[]{:S(2)}) %collective-permute-start.5) | collective-permute-done | bytes 262176 | tf_op jit(solution)/shard_map/while/body/eval_jaxpr/ppermute | solution.py:27
  461.6 5.7 bitcast_dynamic-update-slice_fusion.5
  468.6 9.4 %collective-permute-done.5 = f32[8,2,8,512]{3,0,2,1:T(8,128)S(1)} collective-permute-done((f32[8,2,8,512]{3,0,2,1:T(8,128)S(1)}, f32[8,2,8,512]{3,0,2,1:T(8,128)S(1)}, u32[]{:S(2)}, u32[]{:S(2)}) %collective-permute-start.5) | collective-permute-done | bytes 262176 | tf_op jit(solution)/shard_map/while/body/eval_jaxpr/ppermute | solution.py:27
  478.9 11.1 %psum.14 = f32[32,32]{1,0:T(8,128)S(1)} all-reduce(f32[32,32]{1,0:T(8,128)S(1)} %fusion.62), channel_id=1, replica_groups=mesh['layer'=8,'tile'=4] {'tile'}, use_global_device_ids=true, to_apply=%region_4.5 | all-reduce | flops 1024 | bytes 8192 | tf_op jit(solution)/shard_map/psum | solution.py:143
  490.0 36.0 %psum.15 = f32[32,32]{1,0:T(8,128)S(1)} all-reduce(f32[32,32]{1,0:T(8,128)S(1)} %psum.14), channel_id=1, replica_groups=mesh['layer'=8,'tile'=4] {'layer'}, use_global_device_ids=true, to_apply=%region_5.6 | all-reduce | flops 1024 | bytes 8192 | tf_op jit(solution)/shard_map/psum | solution.py:143
  526.0 58.2 %while.66 = (s32[]{:T(128)}, f32[32,32]{1,0:T(8,128)S(1)}, f32[32,32]{1,0:T(8,128)S(1)}, s32[]{:T(128)}, s32[]{:T(128)}) while((s32[]{:T(128)}, f32[32,32]{1,0:T(8,128)S(1)}, f32[32,32]{1,0:T(8,128)S(1)}, s32[]{:T(128)}, s32[]{:T(128)}) %tuple.180), condition=%wide.region_8.9_spmd.clone.clone, body=%wide.region_6.8_spmd.clone.clone.sunk | while | flops 42338 | bytes 21869 | solution.py:43
  584.2 50.9 %while.65 = (s32[]{:T(128)}, f32[32,32]{1,0:T(8,128)S(1)}, f32[32,32]{1,0:T(8,128)S(1)}, s32[]{:T(128)}, s32[]{:T(128)}) while((s32[]{:T(128)}, f32[32,32]{1,0:T(8,128)S(1)}, f32[32,32]{1,0:T(8,128)S(1)}, s32[]{:T(128)}, s32[]{:T(128)}) %tuple.183), condition=%wide.region_11.12_spmd.clone, body=%wide.region_9.11_spmd.clone.sunk | while | flops 28994 | bytes 17244 | solution.py:57
  (553 shorter events, 293.8 us)
Async XLA Ops:
  3.6 4.5 collective-permute-start
  6.0 5.2 collective-permute-start.1
  17.0 5.9 collective-permute-start.2
  23.0 5.6 collective-permute-start
  26.5 3.5 collective-permute-start.1
  35.8 6.9 %collective-permute-start.2 = (bf16[8,2,8,512]{3,0,2,1:T(8,128)(2,1)S(1)}, bf16[8,2,8,512]{3,0,2,1:T(8,128)(2,1)S(1)}, u32[]{:S(2)}, u32[]{:S(2)}) collective-permute-start(bf16[8,2,8,512]{3,0,2,1:T(8,128)(2,1)S(1)} %bitcast.184), channel_id=1, source_target_pairs={{0,4},{4,8},{8,12},{12,16},{16,20},{20,24},{24,28},{1,5},{5,9},{9,... | collective-permute-start | bytes 393224 | tf_op jit(solution)/shard_map/while/body/eval_jaxpr/ppermute | solution.py:27
  42.7 5.6 collective-permute-start
  55.5 6.9 %collective-permute-start.2 = (bf16[8,2,8,512]{3,0,2,1:T(8,128)(2,1)S(1)}, bf16[8,2,8,512]{3,0,2,1:T(8,128)(2,1)S(1)}, u32[]{:S(2)}, u32[]{:S(2)}) collective-permute-start(bf16[8,2,8,512]{3,0,2,1:T(8,128)(2,1)S(1)} %bitcast.184), channel_id=1, source_target_pairs={{0,4},{4,8},{8,12},{12,16},{16,20},{20,24},{24,28},{1,5},{5,9},{9,... | collective-permute-start | bytes 393224 | tf_op jit(solution)/shard_map/while/body/eval_jaxpr/ppermute | solution.py:27
  62.4 5.6 collective-permute-start
  65.9 3.5 collective-permute-start.1
  75.2 7.8 %collective-permute-start.2 = (bf16[8,2,8,512]{3,0,2,1:T(8,128)(2,1)S(1)}, bf16[8,2,8,512]{3,0,2,1:T(8,128)(2,1)S(1)}, u32[]{:S(2)}, u32[]{:S(2)}) collective-permute-start(bf16[8,2,8,512]{3,0,2,1:T(8,128)(2,1)S(1)} %bitcast.184), channel_id=1, source_target_pairs={{0,4},{4,8},{8,12},{12,16},{16,20},{20,24},{24,28},{1,5},{5,9},{9,... | collective-permute-start | bytes 393224 | tf_op jit(solution)/shard_map/while/body/eval_jaxpr/ppermute | solution.py:27
  83.0 5.6 collective-permute-start
  95.8 7.8 %collective-permute-start.2 = (bf16[8,2,8,512]{3,0,2,1:T(8,128)(2,1)S(1)}, bf16[8,2,8,512]{3,0,2,1:T(8,128)(2,1)S(1)}, u32[]{:S(2)}, u32[]{:S(2)}) collective-permute-start(bf16[8,2,8,512]{3,0,2,1:T(8,128)(2,1)S(1)} %bitcast.184), channel_id=1, source_target_pairs={{0,4},{4,8},{8,12},{12,16},{16,20},{20,24},{24,28},{1,5},{5,9},{9,... | collective-permute-start | bytes 393224 | tf_op jit(solution)/shard_map/while/body/eval_jaxpr/ppermute | solution.py:27
  103.6 5.6 collective-permute-start
  116.4 7.8 %collective-permute-start.2 = (bf16[8,2,8,512]{3,0,2,1:T(8,128)(2,1)S(1)}, bf16[8,2,8,512]{3,0,2,1:T(8,128)(2,1)S(1)}, u32[]{:S(2)}, u32[]{:S(2)}) collective-permute-start(bf16[8,2,8,512]{3,0,2,1:T(8,128)(2,1)S(1)} %bitcast.184), channel_id=1, source_target_pairs={{0,4},{4,8},{8,12},{12,16},{16,20},{20,24},{24,28},{1,5},{5,9},{9,... | collective-permute-start | bytes 393224 | tf_op jit(solution)/shard_map/while/body/eval_jaxpr/ppermute | solution.py:27
  124.2 5.6 collective-permute-start
  127.7 3.5 collective-permute-start.1
  137.0 7.8 %collective-permute-start.2 = (bf16[8,2,8,512]{3,0,2,1:T(8,128)(2,1)S(1)}, bf16[8,2,8,512]{3,0,2,1:T(8,128)(2,1)S(1)}, u32[]{:S(2)}, u32[]{:S(2)}) collective-permute-start(bf16[8,2,8,512]{3,0,2,1:T(8,128)(2,1)S(1)} %bitcast.184), channel_id=1, source_target_pairs={{0,4},{4,8},{8,12},{12,16},{16,20},{20,24},{24,28},{1,5},{5,9},{9,... | collective-permute-start | bytes 393224 | tf_op jit(solution)/shard_map/while/body/eval_jaxpr/ppermute | solution.py:27
  144.8 5.6 collective-permute-start
  157.6 7.8 %collective-permute-start.2 = (bf16[8,2,8,512]{3,0,2,1:T(8,128)(2,1)S(1)}, bf16[8,2,8,512]{3,0,2,1:T(8,128)(2,1)S(1)}, u32[]{:S(2)}, u32[]{:S(2)}) collective-permute-start(bf16[8,2,8,512]{3,0,2,1:T(8,128)(2,1)S(1)} %bitcast.184), channel_id=1, source_target_pairs={{0,4},{4,8},{8,12},{12,16},{16,20},{20,24},{24,28},{1,5},{5,9},{9,... | collective-permute-start | bytes 393224 | tf_op jit(solution)/shard_map/while/body/eval_jaxpr/ppermute | solution.py:27
  165.4 5.6 collective-permute-start
  178.2 7.8 %collective-permute-start.2 = (bf16[8,2,8,512]{3,0,2,1:T(8,128)(2,1)S(1)}, bf16[8,2,8,512]{3,0,2,1:T(8,128)(2,1)S(1)}, u32[]{:S(2)}, u32[]{:S(2)}) collective-permute-start(bf16[8,2,8,512]{3,0,2,1:T(8,128)(2,1)S(1)} %bitcast.184), channel_id=1, source_target_pairs={{0,4},{4,8},{8,12},{12,16},{16,20},{20,24},{24,28},{1,5},{5,9},{9,... | collective-permute-start | bytes 393224 | tf_op jit(solution)/shard_map/while/body/eval_jaxpr/ppermute | solution.py:27
  186.0 5.6 collective-permute-start
  198.8 7.8 %collective-permute-start.2 = (bf16[8,2,8,512]{3,0,2,1:T(8,128)(2,1)S(1)}, bf16[8,2,8,512]{3,0,2,1:T(8,128)(2,1)S(1)}, u32[]{:S(2)}, u32[]{:S(2)}) collective-permute-start(bf16[8,2,8,512]{3,0,2,1:T(8,128)(2,1)S(1)} %bitcast.184), channel_id=1, source_target_pairs={{0,4},{4,8},{8,12},{12,16},{16,20},{20,24},{24,28},{1,5},{5,9},{9,... | collective-permute-start | bytes 393224 | tf_op jit(solution)/shard_map/while/body/eval_jaxpr/ppermute | solution.py:27
  206.6 5.6 collective-permute-start
  219.4 7.8 %collective-permute-start.2 = (bf16[8,2,8,512]{3,0,2,1:T(8,128)(2,1)S(1)}, bf16[8,2,8,512]{3,0,2,1:T(8,128)(2,1)S(1)}, u32[]{:S(2)}, u32[]{:S(2)}) collective-permute-start(bf16[8,2,8,512]{3,0,2,1:T(8,128)(2,1)S(1)} %bitcast.184), channel_id=1, source_target_pairs={{0,4},{4,8},{8,12},{12,16},{16,20},{20,24},{24,28},{1,5},{5,9},{9,... | collective-permute-start | bytes 393224 | tf_op jit(solution)/shard_map/while/body/eval_jaxpr/ppermute | solution.py:27
  227.3 5.6 collective-permute-start.3
  240.1 10.6 %collective-permute-start.5 = (f32[8,2,8,512]{3,0,2,1:T(8,128)S(1)}, f32[8,2,8,512]{3,0,2,1:T(8,128)S(1)}, u32[]{:S(2)}, u32[]{:S(2)}) collective-permute-start(f32[8,2,8,512]{3,0,2,1:T(8,128)S(1)} %get-tuple-element.874), channel_id=1, source_target_pairs={{4,0},{8,4},{12,8},{16,12},{20,16},{24,20},{28,24},{5,1},{9,5},{13... | collective-permute-start | bytes 786440 | tf_op jit(solution)/shard_map/while/body/eval_jaxpr/ppermute | solution.py:27
  250.8 5.6 collective-permute-start.3
  263.2 11.0 %collective-permute-start.5 = (f32[8,2,8,512]{3,0,2,1:T(8,128)S(1)}, f32[8,2,8,512]{3,0,2,1:T(8,128)S(1)}, u32[]{:S(2)}, u32[]{:S(2)}) collective-permute-start(f32[8,2,8,512]{3,0,2,1:T(8,128)S(1)} %get-tuple-element.874), channel_id=1, source_target_pairs={{4,0},{8,4},{12,8},{16,12},{20,16},{24,20},{28,24},{5,1},{9,5},{13... | collective-permute-start | bytes 786440 | tf_op jit(solution)/shard_map/while/body/eval_jaxpr/ppermute | solution.py:27
  274.2 5.3 collective-permute-start.3
  286.3 10.7 %collective-permute-start.5 = (f32[8,2,8,512]{3,0,2,1:T(8,128)S(1)}, f32[8,2,8,512]{3,0,2,1:T(8,128)S(1)}, u32[]{:S(2)}, u32[]{:S(2)}) collective-permute-start(f32[8,2,8,512]{3,0,2,1:T(8,128)S(1)} %get-tuple-element.874), channel_id=1, source_target_pairs={{4,0},{8,4},{12,8},{16,12},{20,16},{24,20},{28,24},{5,1},{9,5},{13... | collective-permute-start | bytes 786440 | tf_op jit(solution)/shard_map/while/body/eval_jaxpr/ppermute | solution.py:27
  297.0 5.1 collective-permute-start.3
  308.9 10.7 %collective-permute-start.5 = (f32[8,2,8,512]{3,0,2,1:T(8,128)S(1)}, f32[8,2,8,512]{3,0,2,1:T(8,128)S(1)}, u32[]{:S(2)}, u32[]{:S(2)}) collective-permute-start(f32[8,2,8,512]{3,0,2,1:T(8,128)S(1)} %get-tuple-element.874), channel_id=1, source_target_pairs={{4,0},{8,4},{12,8},{16,12},{20,16},{24,20},{28,24},{5,1},{9,5},{13... | collective-permute-start | bytes 786440 | tf_op jit(solution)/shard_map/while/body/eval_jaxpr/ppermute | solution.py:27
  319.6 5.1 collective-permute-start.3
  331.5 10.7 %collective-permute-start.5 = (f32[8,2,8,512]{3,0,2,1:T(8,128)S(1)}, f32[8,2,8,512]{3,0,2,1:T(8,128)S(1)}, u32[]{:S(2)}, u32[]{:S(2)}) collective-permute-start(f32[8,2,8,512]{3,0,2,1:T(8,128)S(1)} %get-tuple-element.874), channel_id=1, source_target_pairs={{4,0},{8,4},{12,8},{16,12},{20,16},{24,20},{28,24},{5,1},{9,5},{13... | collective-permute-start | bytes 786440 | tf_op jit(solution)/shard_map/while/body/eval_jaxpr/ppermute | solution.py:27
  342.2 5.1 collective-permute-start.3
  354.1 10.7 %collective-permute-start.5 = (f32[8,2,8,512]{3,0,2,1:T(8,128)S(1)}, f32[8,2,8,512]{3,0,2,1:T(8,128)S(1)}, u32[]{:S(2)}, u32[]{:S(2)}) collective-permute-start(f32[8,2,8,512]{3,0,2,1:T(8,128)S(1)} %get-tuple-element.874), channel_id=1, source_target_pairs={{4,0},{8,4},{12,8},{16,12},{20,16},{24,20},{28,24},{5,1},{9,5},{13... | collective-permute-start | bytes 786440 | tf_op jit(solution)/shard_map/while/body/eval_jaxpr/ppermute | solution.py:27
  364.8 5.1 collective-permute-start.3
  376.8 10.7 %collective-permute-start.5 = (f32[8,2,8,512]{3,0,2,1:T(8,128)S(1)}, f32[8,2,8,512]{3,0,2,1:T(8,128)S(1)}, u32[]{:S(2)}, u32[]{:S(2)}) collective-permute-start(f32[8,2,8,512]{3,0,2,1:T(8,128)S(1)} %get-tuple-element.874), channel_id=1, source_target_pairs={{4,0},{8,4},{12,8},{16,12},{20,16},{24,20},{28,24},{5,1},{9,5},{13... | collective-permute-start | bytes 786440 | tf_op jit(solution)/shard_map/while/body/eval_jaxpr/ppermute | solution.py:27
  387.5 5.1 collective-permute-start.3
  399.4 10.7 %collective-permute-start.5 = (f32[8,2,8,512]{3,0,2,1:T(8,128)S(1)}, f32[8,2,8,512]{3,0,2,1:T(8,128)S(1)}, u32[]{:S(2)}, u32[]{:S(2)}) collective-permute-start(f32[8,2,8,512]{3,0,2,1:T(8,128)S(1)} %get-tuple-element.874), channel_id=1, source_target_pairs={{4,0},{8,4},{12,8},{16,12},{20,16},{24,20},{28,24},{5,1},{9,5},{13... | collective-permute-start | bytes 786440 | tf_op jit(solution)/shard_map/while/body/eval_jaxpr/ppermute | solution.py:27
  410.1 5.1 collective-permute-start.3
  422.0 10.7 %collective-permute-start.5 = (f32[8,2,8,512]{3,0,2,1:T(8,128)S(1)}, f32[8,2,8,512]{3,0,2,1:T(8,128)S(1)}, u32[]{:S(2)}, u32[]{:S(2)}) collective-permute-start(f32[8,2,8,512]{3,0,2,1:T(8,128)S(1)} %get-tuple-element.874), channel_id=1, source_target_pairs={{4,0},{8,4},{12,8},{16,12},{20,16},{24,20},{28,24},{5,1},{9,5},{13... | collective-permute-start | bytes 786440 | tf_op jit(solution)/shard_map/while/body/eval_jaxpr/ppermute | solution.py:27
  432.7 5.1 collective-permute-start.3
  444.6 10.7 %collective-permute-start.5 = (f32[8,2,8,512]{3,0,2,1:T(8,128)S(1)}, f32[8,2,8,512]{3,0,2,1:T(8,128)S(1)}, u32[]{:S(2)}, u32[]{:S(2)}) collective-permute-start(f32[8,2,8,512]{3,0,2,1:T(8,128)S(1)} %get-tuple-element.874), channel_id=1, source_target_pairs={{4,0},{8,4},{12,8},{16,12},{20,16},{24,20},{28,24},{5,1},{9,5},{13... | collective-permute-start | bytes 786440 | tf_op jit(solution)/shard_map/while/body/eval_jaxpr/ppermute | solution.py:27
  455.3 5.1 collective-permute-start.3
  467.3 10.7 %collective-permute-start.5 = (f32[8,2,8,512]{3,0,2,1:T(8,128)S(1)}, f32[8,2,8,512]{3,0,2,1:T(8,128)S(1)}, u32[]{:S(2)}, u32[]{:S(2)}) collective-permute-start(f32[8,2,8,512]{3,0,2,1:T(8,128)S(1)} %get-tuple-element.874), channel_id=1, source_target_pairs={{4,0},{8,4},{12,8},{16,12},{20,16},{24,20},{28,24},{5,1},{9,5},{13... | collective-permute-start | bytes 786440 | tf_op jit(solution)/shard_map/while/body/eval_jaxpr/ppermute | solution.py:27
  (18 other events, 58.5 us)
